TPU v7x, 32 devices: a whole 2x2x4 slice. The times are simulated.
32 devices in a mesh: tx: 2 (over x), ty: 4 (over z), pg: 4 (over y, core).
Axes of the slice: x: 2, y: 2, z: 4, core: 2. Of those that a mesh axis runs over, the one named last changes fastest.
Arguments:
- direct_modes: bfloat16 [64, 3, 32, 512], P('pg', None, 'tx', 'ty'), may hold values from -6 to 6
- adjoint_modes: bfloat16 [64, 3, 32, 512], P(None, None, 'tx', 'ty'), may hold values from -6 to 6
- block_order: int32 [8], replicated, may hold values from 0 to 7, each once
Outputs:
- tensor: float32 [64, 64, 64], P('pg', 'ty', 'tx')
Inputs may be any that keep to these rules, and one draw needn't show every extreme that they name: `block_order`: each of the 8 blocks appears exactly once.
All inputs are finite; a program needn't handle non-finite values.
Results may differ from a plain program's by a relative error of at most 0.0043.
Values may be sent and summed in bfloat16 or wider, within the bound.
A program may use at most 64 MiB of HBM per device.

v0:
```python
import math
import jax
import jax.numpy as jnp
from jax import lax
from jax.sharding import PartitionSpec as P

NBLK = 8
JB = 4
CZ = 4


def extended(block, sides, width):
    for axis, dim in sides:
        count = lax.axis_size(axis)
        forward = [(i, i + 1) for i in range(count - 1)]
        backward = [(target, source) for source, target in forward]
        low = lax.ppermute(
            lax.slice_in_dim(block, block.shape[dim] - width, None, axis=dim), axis, forward
        )
        high = lax.ppermute(lax.slice_in_dim(block, 0, width, axis=dim), axis, backward)
        block = jnp.concatenate([low, block, high], axis=dim)
    return block


def depth_slope(values, depth):
    position = jnp.arange(values.shape[-1]) % depth
    upper = jnp.where(
        position == depth - 1, jnp.roll(values, depth - 1, -1), jnp.roll(values, -1, -1)
    )
    lower = jnp.where(position == 0, jnp.roll(values, 1 - depth, -1), jnp.roll(values, 1, -1))
    return (upper - lower) * 0.5


def slopes(values, wide_x, wide_y, depth):
    along_x = (wide_x[:, :, 2:] - wide_x[:, :, :-2]) * 0.5
    along_y = (wide_y[..., 2 * depth :] - wide_y[..., : -2 * depth]) * 0.5
    along_z = depth_slope(values, depth)
    return jnp.stack([along_x, along_y, along_z], 1).astype(jnp.bfloat16)


def pair_terms(rows_u, rows_g, cols_u, cols_g):
    result = jnp.zeros((rows_u.shape[0], cols_u.shape[0]) + cols_g.shape[2:], jnp.float32)
    for direction in range(3):
        result = result + rows_u[:, None, direction, None] * cols_g[None, :, direction]
        result = result + cols_u[None, :, direction, None] * rows_g[:, None, direction]
    return result.astype(jnp.bfloat16)


def project(pairs, adjoint):
    flat = pairs.reshape(pairs.shape[0] * pairs.shape[1], -1)
    basis = adjoint.reshape(adjoint.shape[0], -1)
    product = lax.dot_general(
        flat, basis, (((1,), (1,)), ((), ())), preferred_element_type=jnp.float32
    )
    return product.reshape(pairs.shape[0], pairs.shape[1], adjoint.shape[0])


def block_tensor(rows_u, rows_g, modes, grads, adjoint, width):
    count = modes.shape[0] // width

    def one_block(start):
        cols_u = lax.dynamic_slice_in_dim(modes, start, width, 0).astype(jnp.float32)
        cols_g = lax.dynamic_slice_in_dim(grads, start, width, 0).astype(jnp.float32)
        return project(pair_terms(rows_u, rows_g, cols_u, cols_g), adjoint)

    starts = jnp.arange(count) * width
    pieces = lax.map(one_block, starts)
    return jnp.transpose(pieces, (1, 0, 2, 3)).reshape(
        rows_u.shape[0], modes.shape[0], adjoint.shape[0]
    )


def shards(direct_modes, adjoint_modes, block_order):
    x_count = lax.axis_size("tx")
    y_count = lax.axis_size("ty")
    group_count = lax.axis_size("pg")
    weight = 1.0 / math.sqrt(
        3.0 * direct_modes.shape[2] * x_count * direct_modes.shape[3] * y_count
    )
    whole = lax.all_gather(direct_modes, "pg", axis=0, tiled=True)
    wide_x = extended(whole, (("tx", 2),), 1)
    wide_y = extended(whole, (("ty", 3),), CZ)
    grads = slopes(
        whole.astype(jnp.float32), wide_x.astype(jnp.float32), wide_y.astype(jnp.float32), CZ
    )
    mode_count = whole.shape[0]
    block_rows = mode_count // NBLK
    per_group = NBLK // group_count
    group_id = lax.axis_index("pg")
    mine = lax.dynamic_slice_in_dim(block_order, group_id * per_group, per_group, 0)
    row_index = (
        mine[:, None] * block_rows + jnp.arange(block_rows, dtype=jnp.int32)[None, :]
    ).reshape(-1)
    rows_u = jnp.take(whole, row_index, axis=0).astype(jnp.float32)
    rows_g = jnp.take(grads, row_index, axis=0).astype(jnp.float32)
    partial_sum = block_tensor(rows_u, rows_g, whole, grads, adjoint_modes, JB) * weight
    row_count = partial_sum.shape[0]
    j_width = mode_count // y_count
    k_width = adjoint_modes.shape[0] // x_count
    arranged = partial_sum.reshape(row_count, y_count, j_width, x_count, k_width)
    arranged = jnp.transpose(arranged, (0, 3, 1, 2, 4)).reshape(row_count, -1)
    shares = lax.psum_scatter(arranged, ("tx", "ty"), scatter_dimension=1, tiled=True)
    return shares.reshape(row_count, j_width, k_width)


def solution(mesh):
    placed = (P("pg", None, "tx", "ty"), P(None, None, "tx", "ty"), P())
    return jax.shard_map(
        shards, mesh=mesh, in_specs=placed, out_specs=P("pg", "ty", "tx"), check_vma=False
    )
```

profile of v0, /device:TPU:0, one launch (start us, length us, event | category | flops | bytes accessed | tf_op | source)
XLA Modules:
  0.0 225.4 jit_solution(8822786861770706708)
XLA Ops:
  6.5 10.3 %all_gather.3 = bf16[64,3,16,128]{3,2,1,0:T(8,128)(2,1)S(1)} all-gather(bf16[16,3,16,128]{3,2,1,0:T(8,128)(2,1)} %param.5), channel_id=1, replica_groups=mesh['tx'=2,'ty'=4,'pg'=4] {'pg'}, dimensions={0}, use_global_device_ids=true | all-gather | bytes 983040 | tf_op jit(solution)/shard_map/all_gather | solution.py:80
  18.4 4.1 %collective-permute-start.2 = (bf16[64,3,16,4]{0,2,3,1:T(8,128)(2,1)}, bf16[64,3,16,4]{0,2,3,1:T(8,128)(2,1)}, u32[]{:S(2)}, u32[]{:S(2)}) collective-permute-start(bf16[64,3,16,4]{0,2,3,1:T(8,128)(2,1)} %copy.25), channel_id=1, source_target_pairs={{0,4},{4,8},{8,12},{1,5},{5,9},{9,13},{2,6},{6,10},{10,14},{3,7},{... | collective-permute-start | bytes 73736 | tf_op jit(solution)/shard_map/ppermute | solution.py:17
  25.9 4.0 %collective-permute-start = (bf16[64,3,1,128]{3,2,1,0:T(2,128)(2,1)}, bf16[64,3,1,128]{3,2,1,0:T(2,128)(2,1)}, u32[]{:S(2)}, u32[]{:S(2)}) collective-permute-start(bf16[64,3,1,128]{3,2,1,0:T(2,128)(2,1)} %get-tuple-element.106), channel_id=1, source_target_pairs={{0,16},{1,17},{2,18},{3,19},{4,20},{5,21},{6,22},{7,23},{8,24},{9,... | collective-permute-start | bytes 147464 | tf_op jit(solution)/shard_map/ppermute | solution.py:17
  30.0 1.5 collective-permute-start.1
  31.6 2.2 slice_bitcast_fusion.12
  33.7 2.1 slice_bitcast_fusion.14
  35.9 2.2 slice_bitcast_fusion.13
  38.1 1.5 fusion.28
  39.9 2.0 copy.29
  41.9 1.8 copy.30
  44.4 1.8 copy.32
  46.9 6.8 %fusion.21 = bf16[64,1,3,16,128]{4,3,2,1,0:T(8,128)(2,1)} fusion(f32[64,1,3,16,125]{4,3,2,0,1:T(8,128)} %get-tuple-element.103, f32[64,1,3,16,3]{4,3,2,0,1:T(8,128)} %get-tuple-element.105, f32[64,1,3,16,1]{4,3,2,0,1:T(8,128)S(1)} %copy-done, f32[64,1,3,16,127]{4,3,2,0,1:T(8,128)} %get-tuple-element.101, f32[64,1,3,16,3]{4,3,2,0,1:T(8,128)} %get-tuple-element.104, ...), kind=kLoop, calls=%fused_computation.52 | loop fusion | flops 3538944 | bytes 7078144 | tf_op jit(solution)/shard_map/convert.2
  54.9 1.5 copy.27
  56.4 1.5 copy.28
  59.3 1.6 maximum_convert_fusion.1
  62.3 1.6 gather_fusion.1
  66.2 82.4 %while.10 = (s32[]{:T(128)}, f32[16,16,4,64]{3,1,2,0:T(8,128)}, f32[16,3,16,128]{3,0,2,1:T(8,128)S(1)}, s32[16]{0:T(128)S(1)}, bf16[64,3,3,16,128]{4,3,2,1,0:T(8...) while((s32[]{:T(128)}, f32[16,16,4,64]{3,1,2,0:T(8,128)}, ...), condition=%wide.region_1.2_spmd, body=%wide.region_0.1_spmd.sunk | while | flops 55148548 | bytes 7307939 | solution.py:67
  85.4 1.5 fusion.32
  100.8 1.5 fusion.32
  116.3 1.5 fusion.32
  131.7 1.5 fusion.32
  147.1 1.5 fusion.32
  152.2 64.9 %reduce-scatter.2.cloned.1.call-done = f32[16,512]{1,0:T(8,128)} async-done(((f32[16,4096]{1,0:T(8,128)}), f32[16,512]{1,0:T(8,128)}) %reduce-scatter.2.cloned.1.call-update) | async-done | bytes 32784 | tf_op jit(solution)/shard_map/reduce_scatter | solution.py:102
  217.1 1.5 reshape.223
  (172 shorter events, 59.9 us)
Async XLA Ops:
  6.5 210.5 %reduce-scatter.2.cloned.1.call-start = ((), (), s32[]{:S(2)}) async-start(), calls=%async_computation.1 | async-start | bytes 294912 | tf_op jit(solution)/shard_map/reduce_scatter | solution.py:102
  18.4 36.5 %collective-permute-start.2 = (bf16[64,3,16,4]{0,2,3,1:T(8,128)(2,1)}, bf16[64,3,16,4]{0,2,3,1:T(8,128)(2,1)}, u32[]{:S(2)}, u32[]{:S(2)}) collective-permute-start(bf16[64,3,16,4]{0,2,3,1:T(8,128)(2,1)} %copy.25), channel_id=1, source_target_pairs={{0,4},{4,8},{8,12},{1,5},{5,9},{9,13},{2,6},{6,10},{10,14},{3,7},{... | collective-permute-start | bytes 73736 | tf_op jit(solution)/shard_map/ppermute | solution.py:17
  23.8 32.6 %collective-permute-start.3 = (bf16[64,3,16,4]{0,2,3,1:T(8,128)(2,1)}, bf16[64,3,16,4]{0,2,3,1:T(8,128)(2,1)}, u32[]{:S(2)}, u32[]{:S(2)}) collective-permute-start(bf16[64,3,16,4]{0,2,3,1:T(8,128)(2,1)} %copy.26), channel_id=1, source_target_pairs={{4,0},{8,4},{12,8},{5,1},{9,5},{13,9},{6,2},{10,6},{14,10},{7,3},{... | collective-permute-start | bytes 73736 | tf_op jit(solution)/shard_map/ppermute | solution.py:20
  25.9 33.3 %collective-permute-start = (bf16[64,3,1,128]{3,2,1,0:T(2,128)(2,1)}, bf16[64,3,1,128]{3,2,1,0:T(2,128)(2,1)}, u32[]{:S(2)}, u32[]{:S(2)}) collective-permute-start(bf16[64,3,1,128]{3,2,1,0:T(2,128)(2,1)} %get-tuple-element.106), channel_id=1, source_target_pairs={{0,16},{1,17},{2,18},{3,19},{4,20},{5,21},{6,22},{7,23},{8,24},{9,... | collective-permute-start | bytes 147464 | tf_op jit(solution)/shard_map/ppermute | solution.py:17
  30.0 29.3 %collective-permute-start.1 = (bf16[64,3,1,128]{3,2,1,0:T(2,128)(2,1)}, bf16[64,3,1,128]{3,2,1,0:T(2,128)(2,1)}, u32[]{:S(2)}, u32[]{:S(2)}) collective-permute-start(bf16[64,3,1,128]{3,2,1,0:T(2,128)(2,1)} %get-tuple-element.107), channel_id=1, source_target_pairs={{16,0},{17,1},{18,2},{19,3},{20,4},{21,5},{22,6},{23,7},{24,8},{25... | collective-permute-start | bytes 147464 | tf_op jit(solution)/shard_map/ppermute | solution.py:20
  38.1 1.5 copy-start.5
  44.4 2.5 %copy-start = (f32[64,1,3,16,1]{4,3,2,0,1:T(8,128)S(1)}, f32[64,1,3,16,1]{4,3,2,0,1:T(8,128)}, u32[]{:S(2)}) copy-start(f32[64,1,3,16,1]{4,3,2,0,1:T(8,128)} %copy.30) | copy-start | bytes 36868
  46.9 7.0 %copy-start.3 = (bf16[64,3,16,128]{3,2,1,0:T(8,128)(2,1)S(1)}, bf16[64,3,16,128]{3,2,1,0:T(8,128)(2,1)}, u32[]{:S(2)}) copy-start(bf16[64,3,16,128]{3,2,1,0:T(8,128)(2,1)} %param.6) | copy-start | bytes 2359300
  60.9 1.1 copy-start.2
  62.3 1.6 copy-start.1
  65.1 1.1 copy-start.4
Sparse Core Ops, SparseCore 0:
  152.3 64.7 reduce-scatter.1
where the time goes:
time: 227 us; the launch traced here: 225 us
  waiting for transfers between devices  64.9 us (29%)
  local copies, waits for them, and re-layouts  42.5 us (19%)
  loops' own time  31.8 us (14%)
  other arithmetic  28.2 us (12%)
  matrix products  23.3 us (10%)
  between operations  13.6 us (6%)
  starting transfers between devices  10.9 us (5%)
  blocking collectives  10.3 us (5%)
    reduce_scatter x1, waiting for transfers between devices, shards(): lax.psum_scatter(arranged, ('tx', 'ty'), scatter_dimension=1, tiled=True)  64.9 us
    another operation x1, loops' own time, block_tensor(): pieces = lax.map(one_block, starts)  31.8 us
    dot_general x16, matrix products, project(): lax.dot_general(flat, basis, (((1,), (1,)), ((), ())), preferred_element_...  23.3 us
    convert_element_type x16, other arithmetic, one_block(): lax.dynamic_slice_in_dim(grads, start, width, 0).astype(jnp.float32)  15 us
    all_gather x1, blocking collectives, shards(): whole = lax.all_gather(direct_modes, 'pg', axis=0, tiled=True)  10.3 us
    dynamic_slice x16, local copies, waits for them, and re-layouts, block_tensor(): pieces = lax.map(one_block, starts)  9.31 us
    ppermute x2, starting transfers between devices, extended(): lax.ppermute(lax.slice_in_dim(block, block.shape[dim] - width, None, axis...  8.12 us
    another operation x1, other arithmetic  6.81 us
  transfers between devices with their start and end apart: 5, of which 1 were waited for; matrix products, arithmetic and copies ran while one was open for 13% of the time, Pallas kernels for 0%

commit v1 on v0

--- a/solution.py
+++ b/solution.py
@@ -7,6 +7,22 @@
 NBLK = 8
 JB = 4
 CZ = 4
+
+
+def gather_around(x, axis, dim):
+    ways, here, step = (lax.axis_size(axis), lax.axis_index(axis), x.shape[dim])
+    shape = [n * ways if d == dim else n for d, n in enumerate(x.shape)]
+    full = lax.dynamic_update_slice_in_dim(jnp.zeros(shape, x.dtype), x, here * step, axis=dim)
+    going_up = going_down = x
+    for far in range(1, ways // 2 + 1):
+        going_up = lax.ppermute(going_up, axis, [(d, (d + 1) % ways) for d in range(ways)])
+        full = lax.dynamic_update_slice_in_dim(full, going_up, (here - far) % ways * step, axis=dim)
+        if 2 * far < ways:
+            going_down = lax.ppermute(going_down, axis, [(d, (d - 1) % ways) for d in range(ways)])
+            full = lax.dynamic_update_slice_in_dim(
+                full, going_down, (here + far) % ways * step, axis=dim
+            )
+    return full
 
 
 def extended(block, sides, width):
@@ -77,7 +93,7 @@
     weight = 1.0 / math.sqrt(
         3.0 * direct_modes.shape[2] * x_count * direct_modes.shape[3] * y_count
     )
-    whole = lax.all_gather(direct_modes, "pg", axis=0, tiled=True)
+    whole = gather_around(direct_modes, "pg", 0)
     wide_x = extended(whole, (("tx", 2),), 1)
     wide_y = extended(whole, (("ty", 3),), CZ)
     grads = slopes(

time: 227 us -> 221 us (0.974)
  blocking collectives: 10.3 us -> 0 us
  waiting for transfers between devices: 64.9 us -> 69.2 us
  starting transfers between devices: 10.9 us -> 15 us
  loops' own time: 31.8 us -> 28.3 us
    all_gather x1 -> x0, blocking collectives: 10.3 us -> none  [shards(): whole = lax.all_gather(direct_modes, 'pg', axis=0, tiled=True)]
    ppermute x0 -> x3, starting transfers between devices: none -> 4.47 us  [the longest x2 2.51 us: gather_around(): lax.ppermute(going_up, axis, [(d, (d + 1) % ways) for d in range(ways)])]
    another operation x1, loops' own time: 31.8 us -> 28.3 us  [block_tensor(): pieces = lax.map(one_block, starts)]
    ppermute x0 -> x3, waiting for transfers between devices: none -> 3.12 us  [the longest x2 3.12 us: gather_around(): lax.ppermute(going_up, axis, [(d, (d + 1) % ways) for d in range(ways)])]
  transfers between devices with their start and end apart: 5 -> 8, of which waited for: 1 -> 3; matrix products, arithmetic and copies ran while one was open for 13% -> 7% of each run, Pallas kernels for 0% -> 0%
where the time goes in v1:
time: 221 us; the launch traced here: 220 us
  waiting for transfers between devices  69.2 us (31%)
  local copies, waits for them, and re-layouts  42.5 us (19%)
  loops' own time  28.3 us (13%)
  other arithmetic  27.8 us (13%)
  matrix products  23.2 us (10%)
  starting transfers between devices  15 us (7%)
  between operations  13.7 us (6%)
    reduce_scatter x1, waiting for transfers between devices, shards(): lax.psum_scatter(arranged, ('tx', 'ty'), scatter_dimension=1, tiled=True)  66 us
    another operation x1, loops' own time, block_tensor(): pieces = lax.map(one_block, starts)  28.3 us
    dot_general x16, matrix products, project(): lax.dot_general(flat, basis, (((1,), (1,)), ((), ())), preferred_element_...  23.2 us
    convert_element_type x16, other arithmetic, one_block(): lax.dynamic_slice_in_dim(grads, start, width, 0).astype(jnp.float32)  15 us
    dynamic_slice x16, local copies, waits for them, and re-layouts, block_tensor(): pieces = lax.map(one_block, starts)  9.41 us
    ppermute x2, starting transfers between devices, extended(): lax.ppermute(lax.slice_in_dim(block, block.shape[dim] - width, None, axis...  7.82 us
    another operation x1, other arithmetic  6.76 us
  transfers between devices with their start and end apart: 8, of which 3 were waited for; matrix products, arithmetic and copies ran while one was open for 7% of the time, Pallas kernels for 0%

profile of v1, /device:TPU:0, one launch (start us, length us, event | category | flops | bytes accessed | tf_op | source)
XLA Modules:
  0.0 219.7 jit_solution(2281152613550214009)
XLA Ops:
  7.0 2.0 collective-permute-start.1
  9.9 2.3 %copy.43 = bf16[64,3,16,128]{3,0,2,1:T(8,128)(2,1)} copy(bf16[64,3,16,128]{3,2,1,0:T(8,128)(2,1)} %param.6) | data formatting | bytes 1572864 | tf_op jit(solution)/shard_map/while | solution.py:83
  12.6 2.1 collective-permute-start.2
  14.7 3.0 %collective-permute-done.2 = bf16[16,3,16,128]{3,2,1,0:T(8,128)(2,1)S(1)} collective-permute-done((bf16[16,3,16,128]{3,2,1,0:T(8,128)(2,1)S(1)}, bf16[16,3,16,128]{3,2,1,0:T(8,128)(2,1)S(1)}, u32[]{:S(2)}, u32[]{:S(2)}) %collective-permute-start.2) | collective-permute-done | bytes 196640 | tf_op jit(solution)/shard_map/ppermute | solution.py:18
  17.7 1.5 fusion.28
  19.3 2.2 slice_bitcast_fusion.12
  21.5 2.1 slice_bitcast_fusion.14
  23.6 2.2 %slice_bitcast_fusion.13 = (f32[64,1,3,16,3]{4,3,2,0,1:T(8,128)}, f32[64,1,3,16,3]{4,3,2,0,1:T(8,128)}) fusion(f32[64,3,16,128]{3,2,1,0:T(8,128)S(1)} %convert_element_type.31), kind=kLoop, calls=%fused_computation.36 | loop fusion | bytes 147456 | tf_op jit(solution)/shard_map/jit(_roll_static)/concatenate | solution.py:46
  27.2 2.0 copy.31
  29.2 1.8 copy.32
  31.7 1.8 copy.34
  33.5 1.8 copy.27
  35.3 4.4 %collective-permute-start.5 = (bf16[64,3,16,4]{0,2,3,1:T(8,128)(2,1)S(1)}, bf16[64,3,16,4]{0,2,3,1:T(8,128)(2,1)S(1)}, u32[]{:S(2)}, u32[]{:S(2)}) collective-permute-start(bf16[64,3,16,4]{0,2,3,1:T(8,128)(2,1)S(1)} %copy.27), channel_id=1, source_target_pairs={{0,4},{4,8},{8,12},{1,5},{5,9},{9,13},{2,6},{6,10},{10,14},{3,7},{... | collective-permute-start | bytes 73736 | tf_op jit(solution)/shard_map/ppermute | solution.py:33
  41.7 3.4 %collective-permute-start.3 = (bf16[64,3,1,128]{3,2,1,0:T(2,128)(2,1)S(1)}, bf16[64,3,1,128]{3,2,1,0:T(2,128)(2,1)S(1)}, u32[]{:S(2)}, u32[]{:S(2)}) collective-permute-start(bf16[64,3,1,128]{3,2,1,0:T(2,128)(2,1)S(1)} %get-tuple-element.106), channel_id=1, source_target_pairs={{0,16},{1,17},{2,18},{3,19},{4,20},{5,21},{6,22},{7,23},{8,24},{9,... | collective-permute-start | bytes 147464 | tf_op jit(solution)/shard_map/ppermute | solution.py:33
  45.1 1.5 collective-permute-start.4
  47.2 6.8 %fusion.21 = bf16[64,1,3,16,128]{4,3,2,1,0:T(8,128)(2,1)} fusion(f32[64,1,3,16,125]{4,3,2,0,1:T(8,128)} %get-tuple-element.103, f32[64,1,3,16,3]{4,3,2,0,1:T(8,128)} %get-tuple-element.105, f32[64,1,3,16,1]{4,3,2,0,1:T(8,128)S(1)} %copy-done, f32[64,1,3,16,127]{4,3,2,0,1:T(8,128)} %get-tuple-element.101, f32[64,1,3,16,3]{4,3,2,0,1:T(8,128)} %get-tuple-element.104, ...), kind=kLoop, calls=%fused_computation.52 | loop fusion | flops 3538944 | bytes 7078144 | tf_op jit(solution)/shard_map/convert.2
  58.9 1.6 gather_fusion.1
  62.8 78.9 %while.10 = (s32[]{:T(128)}, f32[16,16,4,64]{3,1,2,0:T(8,128)}, f32[16,3,16,128]{3,0,2,1:T(8,128)S(1)}, s32[16]{0:T(128)S(1)}, bf16[64,3,3,16,128]{4,3,2,1,0:T(8...) while((s32[]{:T(128)}, f32[16,16,4,64]{3,1,2,0:T(8,128)}, ...), condition=%wide.region_1.2_spmd, body=%wide.region_0.1_spmd.sunk | while | flops 55148548 | bytes 7307939 | solution.py:83
  71.3 1.5 fusion.32
  100.8 1.5 fusion.32
  115.6 1.5 fusion.32
  120.6 1.5 fusion.32
  145.3 66.0 %reduce-scatter.2.cloned.1.call-done = f32[16,512]{1,0:T(8,128)} async-done(((f32[16,4096]{1,0:T(8,128)}), f32[16,512]{1,0:T(8,128)}) %reduce-scatter.2.cloned.1.call-update) | async-done | bytes 32784 | tf_op jit(solution)/shard_map/reduce_scatter | solution.py:118
  211.3 1.5 reshape.223
  (180 shorter events, 62.1 us)
Async XLA Ops:
  6.5 5.8 %copy-start.4 = (bf16[16,3,16,128]{3,2,1,0:T(8,128)(2,1)S(1)}, bf16[16,3,16,128]{3,2,1,0:T(8,128)(2,1)}, u32[]{:S(2)}) copy-start(bf16[16,3,16,128]{3,2,1,0:T(8,128)(2,1)} %param.5) | copy-start | bytes 589828
  6.5 204.8 %reduce-scatter.2.cloned.1.call-start = ((), (), s32[]{:S(2)}) async-start(), calls=%async_computation.1 | async-start | bytes 294912 | tf_op jit(solution)/shard_map/reduce_scatter | solution.py:118
  6.5 6.0 %collective-permute-start = (bf16[16,3,16,128]{3,2,1,0:T(8,128)(2,1)}, bf16[16,3,16,128]{3,2,1,0:T(8,128)(2,1)S(1)}, u32[]{:S(2)}, u32[]{:S(2)}) collective-permute-start(bf16[16,3,16,128]{3,2,1,0:T(8,128)(2,1)} %param.5), channel_id=1, source_target_pairs={{0,1},{1,2},{2,3},{3,0},{4,5},{5,6},{6,7},{7,4},{8,9},{9,10},{10,1... | collective-permute-start | bytes 589832 | tf_op jit(solution)/shard_map/ppermute | solution.py:18
  7.0 7.7 %collective-permute-start.1 = (bf16[16,3,16,128]{3,2,1,0:T(8,128)(2,1)}, bf16[16,3,16,128]{3,2,1,0:T(8,128)(2,1)S(1)}, u32[]{:S(2)}, u32[]{:S(2)}) collective-permute-start(bf16[16,3,16,128]{3,2,1,0:T(8,128)(2,1)} %param.5), channel_id=1, source_target_pairs={{0,3},{1,0},{2,1},{3,2},{4,7},{5,4},{6,5},{7,6},{8,11},{9,8},{10,9... | collective-permute-start | bytes 589832 | tf_op jit(solution)/shard_map/ppermute | solution.py:21
  12.6 5.1 %collective-permute-start.2 = (bf16[16,3,16,128]{3,2,1,0:T(8,128)(2,1)S(1)}, bf16[16,3,16,128]{3,2,1,0:T(8,128)(2,1)S(1)}, u32[]{:S(2)}, u32[]{:S(2)}) collective-permute-start(bf16[16,3,16,128]{3,2,1,0:T(8,128)(2,1)S(1)} %collective-permute-done), channel_id=1, source_target_pairs={{0,1},{1,2},{2,3},{3,0},{4,5},{5,6},{6,7},{7,4},{8,9},{9,10},{10,1... | collective-permute-start | bytes 589832 | tf_op jit(solution)/shard_map/ppermute | solution.py:18
  31.7 15.5 %copy-start = (f32[64,1,3,16,1]{4,3,2,0,1:T(8,128)S(1)}, f32[64,1,3,16,1]{4,3,2,0,1:T(8,128)}, u32[]{:S(2)}) copy-start(f32[64,1,3,16,1]{4,3,2,0,1:T(8,128)} %copy.32) | copy-start | bytes 36868
  35.3 18.9 %collective-permute-start.5 = (bf16[64,3,16,4]{0,2,3,1:T(8,128)(2,1)S(1)}, bf16[64,3,16,4]{0,2,3,1:T(8,128)(2,1)S(1)}, u32[]{:S(2)}, u32[]{:S(2)}) collective-permute-start(bf16[64,3,16,4]{0,2,3,1:T(8,128)(2,1)S(1)} %copy.27), channel_id=1, source_target_pairs={{0,4},{4,8},{8,12},{1,5},{5,9},{9,13},{2,6},{6,10},{10,14},{3,7},{... | collective-permute-start | bytes 73736 | tf_op jit(solution)/shard_map/ppermute | solution.py:33
  40.4 14.5 %collective-permute-start.6 = (bf16[64,3,16,4]{0,2,3,1:T(8,128)(2,1)S(1)}, bf16[64,3,16,4]{0,2,3,1:T(8,128)(2,1)S(1)}, u32[]{:S(2)}, u32[]{:S(2)}) collective-permute-start(bf16[64,3,16,4]{0,2,3,1:T(8,128)(2,1)S(1)} %copy.28), channel_id=1, source_target_pairs={{4,0},{8,4},{12,8},{5,1},{9,5},{13,9},{6,2},{10,6},{14,10},{7,3},{... | collective-permute-start | bytes 73736 | tf_op jit(solution)/shard_map/ppermute | solution.py:36
  41.7 15.2 %collective-permute-start.3 = (bf16[64,3,1,128]{3,2,1,0:T(2,128)(2,1)S(1)}, bf16[64,3,1,128]{3,2,1,0:T(2,128)(2,1)S(1)}, u32[]{:S(2)}, u32[]{:S(2)}) collective-permute-start(bf16[64,3,1,128]{3,2,1,0:T(2,128)(2,1)S(1)} %get-tuple-element.106), channel_id=1, source_target_pairs={{0,16},{1,17},{2,18},{3,19},{4,20},{5,21},{6,22},{7,23},{8,24},{9,... | collective-permute-start | bytes 147464 | tf_op jit(solution)/shard_map/ppermute | solution.py:33
  45.1 11.8 %collective-permute-start.4 = (bf16[64,3,1,128]{3,2,1,0:T(2,128)(2,1)S(1)}, bf16[64,3,1,128]{3,2,1,0:T(2,128)(2,1)S(1)}, u32[]{:S(2)}, u32[]{:S(2)}) collective-permute-start(bf16[64,3,1,128]{3,2,1,0:T(2,128)(2,1)S(1)} %get-tuple-element.107), channel_id=1, source_target_pairs={{16,0},{17,1},{18,2},{19,3},{20,4},{21,5},{22,6},{23,7},{24,8},{25... | collective-permute-start | bytes 147464 | tf_op jit(solution)/shard_map/ppermute | solution.py:36
  57.5 1.1 copy-start.2
  58.9 1.6 copy-start.1
  61.7 1.1 copy-start.3
Sparse Core Ops, SparseCore 0:
  145.4 65.8 reduce-scatter.1
